TPU v7x, 32 devices: a whole 2x2x4 slice. The times are simulated.
32 devices in a mesh: dp: 8 (over z, core), tp: 4 (over y, x).
Axes of the slice: x: 2, y: 2, z: 4, core: 2. Of those that a mesh axis runs over, the one named last changes fastest.
Arguments:
- partials: bfloat16 [4, 1280, 7680], P('tp', 'dp'), may hold values from -1.5 to 1.5
- layer_input: bfloat16 [1920, 1280], P(('dp', 'tp')), may hold values from -6 to 6
- ln_gain: float32 [1280], replicated, may hold values from 0.25 to 1.75
- ln_bias: float32 [1280], replicated, may hold values from -3 to 3
- fc1_weight: bfloat16 [1280, 5120], P(None, 'tp'), may hold values from -0.15625 to 0.15625
- fc1_bias: float32 [5120], P('tp'), may hold values from -3 to 3
- fc2_weight: bfloat16 [1280, 5120], P(None, 'tp'), may hold values from -0.078125 to 0.078125
- row_rank: int32 [1280, 1], P('dp'), may hold values from 0 to 3; in each aligned block of 160 rows (0 to 159, 160 to 319, ...) at most 60 rows name the same one
Outputs:
- early_grads: bfloat16 [1920, 6400], P(('dp', 'tp'))
- fc1_grad: bfloat16 [1280, 5120], P('dp', 'tp')
- fc2_grad: bfloat16 [1280, 5120], P('dp', 'tp')
Inputs may be any that keep to these rules, and one draw needn't show every extreme that they name: `row_rank`: in each aligned block of 160 rows (one data replica) no rank is named by more than 60 rows, a bound that some block reaches.
All inputs are finite; a program needn't handle non-finite values.
Results may differ from a plain program's by a relative error of at most 0.029.
Values may be sent and summed in bfloat16 or wider, within the bound.
A program may use at most 64 MiB of HBM per device.

v0:
```python
import jax
import jax.numpy as jnp
from jax import lax
from jax.sharding import PartitionSpec as P


def gelu_parts(preact):
    normal_cdf = 0.5 * (1.0 + lax.erf(preact * 0.7071067811865476))
    density = jnp.exp(-0.5 * preact * preact) * 0.3989422804014327
    return (preact * normal_cdf, normal_cdf + preact * density)


def slot_matrix(rank_ids, groups, slot_count):
    columns = jnp.arange(groups, dtype=jnp.int32)
    onehot = (rank_ids[:, None] == columns[None, :]).astype(jnp.int32)
    position = jnp.cumsum(onehot, axis=0) - 1
    own_position = jnp.sum(position * onehot, axis=1)
    slot_ids = rank_ids * slot_count + own_position
    targets = jnp.arange(groups * slot_count, dtype=jnp.int32)
    return (targets[:, None] == slot_ids[None, :]).astype(jnp.bfloat16)


def normalize(layer_rows, ln_gain, ln_bias):
    values = layer_rows.astype(jnp.float32)
    row_mean = jnp.mean(values, axis=1, keepdims=True)
    centered = values - row_mean
    row_var = jnp.mean(centered * centered, axis=1, keepdims=True)
    return (centered / jnp.sqrt(row_var + 1e-05) * ln_gain + ln_bias).astype(jnp.bfloat16)


def shards(partials, layer_input, ln_gain, ln_bias, fc1_weight, fc1_bias, fc2_weight, row_rank):
    groups = lax.axis_size("tp")
    replicas = lax.axis_size("dp")
    local_part = partials[0]
    row_count = local_part.shape[0]
    slot_count = layer_input.shape[0]
    feature_width = layer_input.shape[1]
    rank_ids = row_rank[:, 0]
    table = slot_matrix(rank_ids, groups, slot_count)
    normed = normalize(layer_input, ln_gain, ln_bias)
    final_rows = lax.psum(
        local_part[:, :feature_width].astype(jnp.float32).astype(jnp.bfloat16), "tp"
    )
    normed_all = lax.all_gather(normed, "tp", axis=0, tiled=True)
    upstream = jnp.dot(table, final_rows, preferred_element_type=jnp.float32).astype(jnp.bfloat16)
    routed_part = local_part[:, feature_width:]
    summed = lax.psum_scatter(
        routed_part.astype(jnp.float32).astype(jnp.bfloat16), "tp", scatter_dimension=0, tiled=True
    )
    share_rows = summed.shape[0]
    own_index = lax.axis_index("tp")
    owned_ranks = lax.dynamic_slice_in_dim(rank_ids, own_index * share_rows, share_rows, 0)
    dest_mask = (owned_ranks[None, :] == jnp.arange(groups, dtype=jnp.int32)[:, None]).astype(
        jnp.bfloat16
    )
    outgoing = dest_mask[:, :, None] * summed[None, :, :]
    incoming = lax.all_to_all(outgoing, "tp", split_axis=0, concat_axis=0, tiled=True).reshape(
        row_count, routed_part.shape[1]
    )
    own_table = lax.dynamic_slice_in_dim(table, own_index * slot_count, slot_count, 0)
    placed = jnp.dot(own_table, incoming, preferred_element_type=jnp.float32).astype(jnp.bfloat16)
    preact = jnp.dot(normed_all, fc1_weight, preferred_element_type=jnp.float32) + fc1_bias
    activated, derivative = gelu_parts(preact)
    hidden = activated.astype(jnp.bfloat16)
    hidden_grad = jnp.dot(upstream, fc2_weight, preferred_element_type=jnp.float32)
    preact_grad = (hidden_grad * derivative).astype(jnp.bfloat16)
    factor = float(replicas * row_count) ** (-0.5)
    grad_first = jnp.dot(normed_all.T, preact_grad, preferred_element_type=jnp.float32) * factor
    grad_second = jnp.dot(upstream.T, hidden, preferred_element_type=jnp.float32) * factor
    reduced = (
        lax.psum_scatter(
            grad_first.astype(jnp.bfloat16), "dp", scatter_dimension=0, tiled=True
        ).astype(jnp.float32),
        lax.psum_scatter(
            grad_second.astype(jnp.bfloat16), "dp", scatter_dimension=0, tiled=True
        ).astype(jnp.float32),
    )
    return (placed, reduced[0].astype(jnp.bfloat16), reduced[1].astype(jnp.bfloat16))


def solution(mesh):
    return jax.shard_map(
        shards,
        mesh=mesh,
        in_specs=(
            P("tp", "dp", None),
            P(("dp", "tp"), None),
            P(),
            P(),
            P(None, "tp"),
            P("tp"),
            P(None, "tp"),
            P("dp", None),
        ),
        out_specs=(P(("dp", "tp"), None), P("dp", "tp"), P("dp", "tp")),
        check_vma=False,
    )
```

profile of v0, /device:TPU:0, one launch (start us, length us, event | category | flops | bytes accessed | tf_op | source)
XLA Modules:
  0.0 192.5 jit_solution(12191497588803698342)
XLA Ops:
  7.2 0.0 copy-start
  7.2 0.0 all-reduce.4.cloned.1.call-start
  7.2 1.9 %slice.23 = bf16[160,1280]{1,0:T(8,128)(2,1)} slice(bf16[160,7680]{1,0:T(8,128)(2,1)} %bitcast.25), slice={[0:160], [0:1280]} | slice | bytes 819200 | tf_op jit(solution)/shard_map/slice | solution.py:42
  9.2 0.0 all-reduce.4.cloned.1.call-update
  9.2 0.0 reduce-scatter.10.cloned.1.call-start
  9.2 3.0 %slice.22 = bf16[160,6400]{1,0:T(8,128)(2,1)} slice(bf16[160,7680]{1,0:T(8,128)(2,1)} %bitcast.26), slice={[0:160], [1280:7680]} | slice | bytes 4096000 | tf_op jit(solution)/shard_map/slice | solution.py:46
  12.3 0.0 copy-start.2
  12.3 0.0 copy-start.1
  12.3 0.0 copy-start.3
  12.3 0.0 copy-start.4
  12.3 0.0 reduce-scatter.10.cloned.1.call-update
  12.3 0.0 reduce-scatter.6.cloned.1.call-start
  12.3 0.6 copy-done.2
  13.0 1.2 reduce-window.6
  14.2 0.1 slice.20
  14.3 0.1 copy.15
  14.4 0.1 copy.16
  14.5 0.1 add_bitcast_fusion
  14.6 0.0 copy-done.1
  14.6 0.1 convert_reduce_fusion
  14.7 0.2 fusion.11
  14.9 0.0 copy-start.5
  15.0 0.0 copy-done.3
  15.0 0.0 copy-done.4
  15.0 0.1 fusion.15
  15.1 14.9 %all-gather = bf16[4,60,1280]{2,1,0:T(8,128)(2,1)} all-gather(bf16[1,60,1280]{2,1,0:T(8,128)(2,1)S(1)} %fusion.15), channel_id=1, replica_groups=mesh['dp'=8,'tp'=4] {'tp'}, dimensions={0}, use_global_device_ids=true | all-gather | bytes 768000 | tf_op jit(solution)/shard_map/all_gather | solution.py:44
  30.1 2.0 %reshape.72 = bf16[240,1280]{1,0:T(8,128)(2,1)} reshape(bf16[4,60,1280]{2,1,0:T(8,128)(2,1)} %all-gather) | data formatting | bytes 1228800
  32.1 0.0 copy-done.5
  32.1 4.2 %convolution_add_fusion = f32[240,1280]{1,0:T(8,128)} fusion(bf16[240,1280]{1,0:T(8,128)(2,1)} %reshape.72, bf16[1280,1280]{1,0:T(8,128)(2,1)} %param.12, f32[1280]{0:T(1024)S(1)} %copy-done.5), kind=kOutput, calls=%fused_computation.6 | convolution fusion | flops 786739200 | bytes 5125120 | tf_op jit(solution)/shard_map/dot_general | solution.py:62
  36.3 23.8 %all-reduce.4.cloned.1.call-done = bf16[160,1280]{1,0:T(8,128)(2,1)} async-done(((bf16[160,1280]{1,0:T(8,128)(2,1)}), bf16[160,1280]{1,0:T(8,128)(2,1)}) %all-reduce.4.cloned.1.call-update) | async-done | bytes 409616 | tf_op jit(solution)/shard_map/psum | solution.py:41
  60.1 2.1 %convolution_convert_fusion.1 = bf16[240,1280]{1,0:T(8,128)(2,1)} fusion(bf16[160,1280]{1,0:T(8,128)(2,1)} %all-reduce.4.cloned.1.call-done, s32[160]{0:T(256)S(1)} %multiply_add_fusion), kind=kOutput, calls=%fused_computation.7 | convolution fusion | flops 98649600 | bytes 1024640 | tf_op jit(solution)/shard_map/dot_general | solution.py:45
  62.2 0.0 copy-done
  62.3 5.2 %fusion = bf16[1280,1280]{1,0:T(8,128)(2,1)} fusion(bf16[240,1280]{1,0:T(8,128)(2,1)} %reshape.72, bf16[240,1280]{1,0:T(8,128)(2,1)} %convolution_convert_fusion.1, bf16[1280,1280]{1,0:T(8,128)(2,1)S(1)} %copy-done, f32[240,1280]{1,0:T(8,128)} %convolution_add_fusion), kind=kOutput, calls=%fused_computation.3 | convolution fusion | flops 1579212800 | bytes 9011200 | tf_op jit(solution)/shard_map/dot_general | solution.py:68
  67.5 0.0 reduce-scatter.6.cloned.1.call-update
  67.5 0.0 reduce-scatter.8.cloned.1.call-start
  67.5 4.3 %fusion.1 = bf16[1280,1280]{1,0:T(8,128)(2,1)} fusion(bf16[240,1280]{1,0:T(8,128)(2,1)} %convolution_convert_fusion.1, f32[240,1280]{1,0:T(8,128)} %convolution_add_fusion), kind=kOutput, calls=%fused_computation.4 | convolution fusion | flops 791244800 | bytes 5120000 | tf_op jit(solution)/shard_map/dot_general | solution.py:69
  71.8 0.0 reduce-scatter.8.cloned.1.call-update
  71.8 0.1 dynamic-slice_bitcast_fusion
  71.9 26.9 %reduce-scatter.10.cloned.1.call-done = bf16[40,6400]{1,0:T(8,128)(2,1)} async-done(((bf16[160,6400]{1,0:T(8,128)(2,1)}), bf16[40,6400]{1,0:T(8,128)(2,1)}) %reduce-scatter.10.cloned.1.call-update) | async-done | bytes 512016
  98.8 2.6 %broadcast_multiply_fusion = bf16[4,40,6400]{2,1,0:T(8,128)(2,1)} fusion(bf16[40,6400]{1,0:T(8,128)(2,1)} %reduce-scatter.10.cloned.1.call-done, bf16[4,40]{1,0:T(4,128)(2,1)S(1)} %fusion.19), kind=kLoop, calls=%fused_computation.16 | loop fusion | flops 1024000 | bytes 2560320 | tf_op jit(solution)/shard_map/mul | solution.py:56
  101.4 4.5 %all-to-all-start = ((bf16[4,40,6400]{2,1,0:T(8,128)(2,1)}), bf16[4,40,6400]{2,1,0:T(8,128)(2,1)}, u32[]{:S(2)}, u32[]{:S(2)}) async-start(bf16[4,40,6400]{2,1,0:T(8,128)(2,1)} %broadcast_multiply_fusion), calls=%async_computation | async-start | bytes 4096000 | tf_op jit(solution)/shard_map/all_to_all | solution.py:57
  105.9 24.5 %all-to-all-done = bf16[4,40,6400]{2,1,0:T(8,128)(2,1)} async-done(((bf16[4,40,6400]{2,1,0:T(8,128)(2,1)}), bf16[4,40,6400]{2,1,0:T(8,128)(2,1)}, u32[]{:S(2)}, u32[]{:S(2)}) %all-to-all-start) | async-done | bytes 2048032 | tf_op jit(solution)/shard_map/all_to_all | solution.py:57
  130.4 2.9 %convolution_convert_fusion = bf16[60,6400]{1,0:T(8,128)(2,1)} fusion(bf16[160,6400]{1,0:T(8,128)(2,1)} %bitcast.5, pred[240,160]{1,0:T(8,128)(4,1)S(1)} %iota_compare_fusion, s32[]{:T(128)S(6)} %select_n.6), kind=kOutput, calls=%fused_computation.2 | convolution fusion | flops 123264000 | bytes 2832388 | tf_op jit(solution)/shard_map/dot_general | solution.py:61
  133.3 9.7 %reduce-scatter.6.cloned.1.call-done = bf16[160,1280]{1,0:T(8,128)(2,1)} async-done(((bf16[1280,1280]{1,0:T(8,128)(2,1)}), bf16[160,1280]{1,0:T(8,128)(2,1)}) %reduce-scatter.6.cloned.1.call-update) | async-done | bytes 409616 | tf_op jit(solution)/shard_map/reduce_scatter | solution.py:71
  143.0 43.0 %reduce-scatter.8.cloned.1.call-done = bf16[160,1280]{1,0:T(8,128)(2,1)} async-done(((bf16[1280,1280]{1,0:T(8,128)(2,1)}), bf16[160,1280]{1,0:T(8,128)(2,1)}) %reduce-scatter.8.cloned.1.call-update) | async-done | bytes 409616 | tf_op jit(solution)/shard_map/reduce_scatter | solution.py:74
  (12 shorter events, 0.2 us)
Async XLA Ops:
  7.2 55.1 %copy-start = (bf16[1280,1280]{1,0:T(8,128)(2,1)S(1)}, bf16[1280,1280]{1,0:T(8,128)(2,1)}, u32[]{:S(2)}) copy-start(bf16[1280,1280]{1,0:T(8,128)(2,1)} %param.14) | copy-start | bytes 9830404
  7.2 52.9 %all-reduce.4.cloned.1.call-start = ((), (), s32[]{:S(2)}) async-start(), calls=%async_computation.4 | async-start | bytes 819200 | tf_op jit(solution)/shard_map/psum | solution.py:41
  9.2 89.6 %reduce-scatter.10.cloned.1.call-start = ((), (), s32[]{:S(2)}) async-start(), calls=%async_computation.7 | async-start | bytes 2560000
  12.3 0.7 copy-start.2
  12.3 2.3 %copy-start.1 = (bf16[60,1280]{1,0:T(8,128)(2,1)S(1)}, bf16[60,1280]{1,0:T(8,128)(2,1)}, u32[]{:S(2)}) copy-start(bf16[60,1280]{1,0:T(8,128)(2,1)} %param.9) | copy-start | bytes 460804
  12.3 2.7 %copy-start.3 = (f32[1280]{0:T(1024)S(1)}, f32[1280]{0:T(1024)}, u32[]{:S(2)}) copy-start(f32[1280]{0:T(1024)} %param.11) | copy-start | bytes 15364
  12.3 2.7 %copy-start.4 = (f32[1280]{0:T(1024)S(1)}, f32[1280]{0:T(1024)}, u32[]{:S(2)}) copy-start(f32[1280]{0:T(1024)} %param.10) | copy-start | bytes 15364
  12.3 130.7 %reduce-scatter.6.cloned.1.call-start = ((), (), s32[]{:S(2)}) async-start(), calls=%async_computation.5 | async-start | bytes 3686400 | tf_op jit(solution)/shard_map/reduce_scatter | solution.py:71
  14.9 17.2 %copy-start.5 = (f32[1280]{0:T(1024)S(1)}, f32[1280]{0:T(1024)}, u32[]{:S(2)}) copy-start(f32[1280]{0:T(1024)} %param.13) | copy-start | bytes 15364
  67.5 118.5 %reduce-scatter.8.cloned.1.call-start = ((), (), s32[]{:S(2)}) async-start(), calls=%async_computation.6 | async-start | bytes 3686400 | tf_op jit(solution)/shard_map/reduce_scatter | solution.py:74
  101.4 29.0 %all-to-all-start = ((bf16[4,40,6400]{2,1,0:T(8,128)(2,1)}), bf16[4,40,6400]{2,1,0:T(8,128)(2,1)}, u32[]{:S(2)}, u32[]{:S(2)}) async-start(bf16[4,40,6400]{2,1,0:T(8,128)(2,1)} %broadcast_multiply_fusion), calls=%async_computation | async-start | bytes 4096000 | tf_op jit(solution)/shard_map/all_to_all | solution.py:57
Sparse Core Ops, SparseCore 0:
  11.6 48.4 all-reduce.3
  63.2 35.5 reduce-scatter.9
  101.7 41.2 reduce-scatter.5
  145.7 40.2 reduce-scatter.7
where the time goes:
time: 193 us; the launch traced here: 192 us
  waiting for transfers between devices  128 us (66%)
  matrix products  18.7 us (10%)
  blocking collectives  14.9 us (8%)
  between operations  13.9 us (7%)
  local copies, waits for them, and re-layouts  7.99 us (4%)
  starting transfers between devices  4.63 us (2%)
  other arithmetic  4.51 us (2%)
    reduce_scatter x1, waiting for transfers between devices, shards(): lax.psum_scatter(grad_second.astype(jnp.bfloat16), 'dp', scatter_dimensio...  43 us
    unnamed x5, waiting for transfers between devices  26.9 us
    all_to_all x1, waiting for transfers between devices, shards(): lax.all_to_all(outgoing, 'tp', split_axis=0, concat_axis=0, tiled=True)  24.5 us
    psum x1, waiting for transfers between devices, shards(): lax.psum(local_part[:, :feature_width].astype(jnp.float32).astype(jnp.bfl...  23.8 us
    all_gather x1, blocking collectives, shards(): normed_all = lax.all_gather(normed, 'tp', axis=0, tiled=True)  14.9 us
    reduce_scatter x1, waiting for transfers between devices, shards(): lax.psum_scatter(grad_first.astype(jnp.bfloat16), 'dp', scatter_dimension...  9.67 us
    dot_general x1, matrix products, shards(): jnp.dot(normed_all.T, preact_grad, preferred_element_type=jnp.float32)  5.2 us
    all_to_all x1, starting transfers between devices, shards(): lax.all_to_all(outgoing, 'tp', split_axis=0, concat_axis=0, tiled=True)  4.46 us
  transfers between devices with their start and end apart: 5, of which 5 were waited for; matrix products, arithmetic and copies ran while one was open for 15% of the time, Pallas kernels for 0%

commit v1 on v0

v1 whole, which is shorter than its diff:
```python
import functools

import jax
import jax.numpy as jnp
from jax import lax
from jax.experimental import pallas as pl
from jax.experimental.pallas import tpu as pltpu
from jax.sharding import PartitionSpec as P

MESH = pl.DeviceIdType.MESH
CORES = 2
F32 = jnp.float32
BF16 = jnp.bfloat16


def up_to(value, step):
    return -(-value // step) * step


def onehot(rows, columns, wanted, axis):
    at = lax.broadcasted_iota(jnp.int32, (rows, columns), axis).astype(F32)
    return jnp.where(at == wanted, 1.0, 0.0).astype(BF16)


def fdot(left, right):
    return jnp.dot(left, right, preferred_element_type=F32)


def kernel(
    n_tp, n_dp, share, factor,
    rank_row, rank_col, part, lin, gain, bias, fc1, b1, fc2,
    early_o, g1_o, g2_o,
    partu, parte, w1, w2, linall, usend, urecv, uall, esend, erecv,
    hidden, deriv, nts, ntr, upt, terms, cross, chain, grads,
    lsem, tsem, dsem, zsem,
):
    me_tp = lax.axis_index("tp")
    me_dp = lax.axis_index("dp")
    z, core = me_dp // CORES, me_dp % CORES
    nz = n_dp // CORES
    partner = {"dp": z * CORES + 1 - core}
    rows, width = partu.shape
    slot_pad = lin.shape[0]
    share_pad = usend.shape[1]
    hid = w1.shape[1]
    depth = g1_o.shape[0]
    step_h = 256 if hid % 256 == 0 else hid

    loads = [
        pltpu.make_async_copy(part.at[:, pl.ds(0, width)], partu, lsem.at[0]),
        pltpu.make_async_copy(part.at[:, pl.ds(width, parte.shape[1])], parte, lsem.at[1]),
        pltpu.make_async_copy(fc1, w1, lsem.at[2]),
        pltpu.make_async_copy(fc2, w2, lsem.at[3]),
    ]
    for load in loads:
        load.start()

    barrier = pltpu.get_barrier_semaphore()
    for i in range(1, n_tp):
        pl.semaphore_signal(barrier, inc=1, device_id={"tp": (me_tp + i) % n_tp}, device_id_type=MESH)
    for i in range(1, n_dp):
        pl.semaphore_signal(barrier, inc=1, device_id={"dp": (me_dp + i) % n_dp}, device_id_type=MESH)
    pl.semaphore_wait(barrier, n_tp + n_dp - 2)

    def remote(src, dst, send, recv, device):
        return pltpu.make_async_remote_copy(
            src_ref=src, dst_ref=dst, send_sem=send, recv_sem=recv, device_id=device, device_id_type=MESH
        )

    def tp_send(src_of, dst, kind):
        for i in range(1, n_tp):
            to = (me_tp + i) % n_tp
            remote(src_of(to), dst.at[me_tp], tsem.at[kind, to], tsem.at[kind + 1, me_tp], {"tp": to}).start()

    def tp_wait(src_of, dst, kind, recv):
        for i in range(1, n_tp):
            to = (me_tp + i) % n_tp
            copy = remote(src_of(to), dst.at[to], tsem.at[kind, to], tsem.at[kind + 1, to], {"tp": to})
            if recv:
                copy.wait_recv()
            else:
                copy.wait_send()

    own_lin = lambda to: lin
    u_block = lambda to: usend.at[to]
    own_up = lambda to: uall.at[me_tp]
    e_block = lambda to: esend.at[to]

    r_row = lax.broadcasted_iota(jnp.int32, (1, rows), 1)
    r_col = lax.broadcasted_iota(jnp.int32, (rows, 1), 0)
    pad_row, pad_col = (r_row * 0).astype(F32), (r_col * 0).astype(F32)
    for i in range(1, n_tp):
        pad_row = pad_row + jnp.where(r_row >= i * share, 1.0, 0.0)
        pad_col = pad_col + jnp.where(r_col >= i * share, 1.0, 0.0)
    pad_row = r_row.astype(F32) + pad_row * (share_pad - share)
    pad_col = r_col.astype(F32) + pad_col * (share_pad - share)

    loads[0].wait()
    spread = onehot(n_tp * share_pad, rows, pad_row, 0)
    usend[...] = fdot(spread, partu[...]).astype(BF16).reshape(usend.shape)
    tp_send(u_block, urecv, 0)
    tp_send(own_lin, linall, 4)
    linall[me_tp] = lin[...]

    rank_r, rank_c = rank_row[...], rank_col[...]
    same = rank_c == rank_r
    at0 = lax.broadcasted_iota(jnp.int32, (rows, rows), 0)
    at1 = lax.broadcasted_iota(jnp.int32, (rows, rows), 1)
    place_r = jnp.sum(jnp.where(same & (at0 < at1), 1.0, 0.0), axis=0, keepdims=True)
    place_c = jnp.sum(jnp.where(same & (at1 < at0), 1.0, 0.0), axis=1, keepdims=True)
    slot_r = rank_r.astype(F32) * slot_pad + place_r
    slot_c = rank_c.astype(F32) * slot_pad + place_c
    table = onehot(n_tp * slot_pad, rows, slot_r, 0)
    back = onehot(rows, n_tp * slot_pad, slot_c, 1)

    loads[1].wait()

    def place(i, carry):
        columns = pl.ds(pl.multiple_of(i * width, 128), width)
        placed = fdot(table, parte[:, columns]).astype(BF16)
        esend[:, :, columns] = placed.reshape(n_tp, slot_pad, width)
        return carry

    lax.fori_loop(0, parte.shape[1] // width, place, 0)

    tp_wait(u_block, urecv, 0, True)
    total = usend[me_tp].astype(F32)
    for i in range(1, n_tp):
        total = total + urecv[(me_tp + i) % n_tp].astype(F32)
    uall[me_tp] = total.astype(BF16)
    tp_send(own_up, uall, 2)
    tp_send(e_block, erecv, 6)

    tp_wait(own_lin, linall, 4, True)
    values = fdot(back, linall[...].reshape(n_tp * slot_pad, width))
    centered = values - jnp.mean(values, axis=1, keepdims=True)
    variance = jnp.mean(centered * centered, axis=1, keepdims=True)
    normed = centered / jnp.sqrt(variance + 1e-05) * gain[...] + bias[...]
    normed_t = jnp.transpose(normed)
    for d in range(n_dp):
        nts[d] = normed_t[d * depth : (d + 1) * depth].astype(BF16)
    normed = normed.astype(BF16)
    for i in range(1, n_dp):
        to = (me_dp + i) % n_dp
        remote(nts.at[to], ntr.at[me_dp], dsem.at[0, to], dsem.at[1, me_dp], {"dp": to}).start()
    ntr[me_dp] = nts[me_dp]

    loads[2].wait()

    def forward(i, carry):
        columns = pl.ds(pl.multiple_of(i * step_h, step_h), step_h) if step_h != hid else slice(None)
        preact = fdot(normed, w1[:, columns]) + b1[:, columns]
        cdf = 0.5 * (1.0 + lax.erf(preact * 0.7071067811865476))
        density = jnp.exp(-0.5 * preact * preact) * 0.3989422804014327
        hidden[:, columns] = (preact * cdf).astype(BF16)
        deriv[:, columns] = cdf + preact * density
        return carry

    lax.fori_loop(0, hid // step_h, forward, 0)

    loads[3].wait()
    tp_wait(own_up, uall, 2, True)
    gather = onehot(rows, n_tp * share_pad, pad_col, 1)
    up_f = fdot(gather, uall[...].reshape(n_tp * share_pad, width))
    up = up_f.astype(BF16)

    def backward(i, carry):
        columns = pl.ds(pl.multiple_of(i * step_h, step_h), step_h) if step_h != hid else slice(None)
        grads[me_dp, :, columns] = (fdot(up, w2[:, columns]) * deriv[:, columns]).astype(BF16)
        return carry

    lax.fori_loop(0, hid // step_h, backward, 0)

    spots = (z, nz - 1 - z)
    ahead = ({"dp": (z + 1) * CORES + core}, {"dp": (z - 1) * CORES + core})

    def real(way, at):
        return at if way == 0 else nz - 1 - at

    def block_copy(way, chip):
        block = grads.at[chip * CORES + core]
        return remote(block, block, zsem.at[way, chip], zsem.at[2 + way, chip], ahead[way])

    def chain_copy(way, owner):
        block = chain.at[way, owner]
        return remote(block, block, zsem.at[4 + way, owner], zsem.at[6 + way, owner], ahead[way])

    def partner_copy(chip, side):
        block = grads.at[chip * CORES + side]
        return remote(block, block, zsem.at[8, chip], zsem.at[9, chip], partner)

    def cross_copy(chip):
        return remote(
            terms.at[chip * CORES + 1 - core], cross.at[chip], zsem.at[10, chip], zsem.at[11, chip], partner
        )

    def send_block(step):
        for way in (0, 1):
            @pl.when((spots[way] >= step) & (spots[way] < nz - 1))
            def _():
                block_copy(way, real(way, spots[way] - step)).start()

    send_block(0)
    partner_copy(z, core).start()

    up_t = jnp.transpose(up_f)
    for d in range(n_dp):
        upt[d] = up_t[d * depth : (d + 1) * depth].astype(BF16)

    def term(d):
        terms[d] = (fdot(upt[d], hidden[...]) * factor).astype(BF16)

    def other_terms(chip, carry):
        term(chip * CORES + 1 - core)
        cross_copy(chip).start()
        return carry

    def own_terms(chip, carry):
        term(chip * CORES + core)
        return carry

    lax.fori_loop(0, nz, other_terms, 0)
    lax.fori_loop(0, nz, own_terms, 0)

    def merge(chip, carry):
        cross_copy(chip).wait_recv()
        own = terms[chip * CORES + core].astype(F32)
        cross[chip] = (own + cross[chip].astype(F32)).astype(BF16)
        return carry

    lax.fori_loop(0, nz, merge, 0)

    for step in range(nz - 1):
        if step:
            send_block(step)
        for way in (0, 1):
            spot = spots[way]
            owner = real(way, nz - 1 + spot - step)

            @pl.when((spot <= step) & (spot == 0))
            def _():
                chain[way, owner] = cross[owner]
                chain_copy(way, owner).start()

            @pl.when((spot <= step) & (spot > 0))
            def _():
                chain_copy(way, owner).wait_recv()
                chain[way, owner] = (chain[way, owner].astype(F32) + cross[owner].astype(F32)).astype(BF16)
                chain_copy(way, owner).start()

        for way in (0, 1):
            @pl.when(spots[way] > step)
            def _():
                chip = real(way, spots[way] - 1 - step)
                block_copy(way, chip).wait_recv()
                partner_copy(chip, core).start()

    tp_wait(e_block, erecv, 6, True)

    def collect(i, carry):
        columns = pl.ds(pl.multiple_of(i * width, 128), width)
        early = esend[me_tp, :, columns].astype(F32)
        for j in range(1, n_tp):
            early = early + erecv[(me_tp + j) % n_tp, :, columns].astype(F32)
        early_o[:, columns] = early.astype(BF16)
        return carry

    lax.fori_loop(0, parte.shape[1] // width, collect, 0)

    for i in range(1, n_dp):
        to = (me_dp + i) % n_dp
        remote(nts.at[to], ntr.at[to], dsem.at[0, to], dsem.at[1, to], {"dp": to}).wait_recv()

    for chip in range(nz):
        partner_copy(chip, 1 - core).wait_recv()
    first = fdot(ntr[0], grads[0])
    for k in range(1, n_dp):
        first = first + fdot(ntr[k], grads[k])
    g1_o[...] = (first * factor).astype(BF16)

    for way in (0, 1):
        @pl.when(spots[way] > 0)
        def _():
            chain_copy(way, z).wait_recv()

        @pl.when(spots[way] == 0)
        def _():
            chain[way, z] = jnp.zeros_like(chain[way, z])

    second = cross[z].astype(F32) + chain[0, z].astype(F32) + chain[1, z].astype(F32)
    g2_o[...] = second.astype(BF16)

    tp_wait(u_block, urecv, 0, False)
    tp_wait(own_up, uall, 2, False)
    tp_wait(own_lin, linall, 4, False)
    tp_wait(e_block, erecv, 6, False)
    for i in range(1, n_dp):
        to = (me_dp + i) % n_dp
        remote(nts.at[to], ntr.at[to], dsem.at[0, to], dsem.at[1, to], {"dp": to}).wait_send()
    for chip in range(nz):
        partner_copy(chip, core).wait_send()
        cross_copy(chip).wait_send()
    for step in range(nz - 1):
        for way in (0, 1):
            spot = spots[way]

            @pl.when((spot >= step) & (spot < nz - 1))
            def _():
                block_copy(way, real(way, spot - step)).wait_send()

            @pl.when(spot <= step)
            def _():
                chain_copy(way, real(way, nz - 1 + spot - step)).wait_send()


def shards(partials, layer_input, ln_gain, ln_bias, fc1_weight, fc1_bias, fc2_weight, row_rank):
    n_tp = lax.axis_size("tp")
    n_dp = lax.axis_size("dp")
    nz = n_dp // CORES
    part = partials[0]
    rows, vis = part.shape
    slots, width = layer_input.shape
    hid = fc1_weight.shape[1]
    slot_pad = up_to(slots, 16)
    share = -(-rows // n_tp)
    share_pad = up_to(share, 16)
    depth = width // n_dp
    rest = vis - width
    vmem = pl.BlockSpec(memory_space=pltpu.VMEM)
    anywhere = pl.BlockSpec(memory_space=pl.ANY)
    padded = jnp.pad(layer_input, ((0, slot_pad - slots), (0, 0)))
    early, first, second = pl.pallas_call(
        functools.partial(kernel, n_tp, n_dp, share, float(n_dp * rows) ** (-0.5)),
        out_shape=(
            jax.ShapeDtypeStruct((slot_pad, rest), BF16),
            jax.ShapeDtypeStruct((depth, hid), BF16),
            jax.ShapeDtypeStruct((depth, hid), BF16),
        ),
        in_specs=[vmem, vmem, anywhere, vmem, vmem, vmem, anywhere, vmem, anywhere],
        out_specs=(vmem, vmem, vmem),
        scratch_shapes=[
            pltpu.VMEM((rows, width), BF16),
            pltpu.VMEM((rows, rest), BF16),
            pltpu.VMEM((width, hid), BF16),
            pltpu.VMEM((width, hid), BF16),
            pltpu.VMEM((n_tp, slot_pad, width), BF16),
            pltpu.VMEM((n_tp, share_pad, width), BF16),
            pltpu.VMEM((n_tp, share_pad, width), BF16),
            pltpu.VMEM((n_tp, share_pad, width), BF16),
            pltpu.VMEM((n_tp, slot_pad, rest), BF16),
            pltpu.VMEM((n_tp, slot_pad, rest), BF16),
            pltpu.VMEM((rows, hid), BF16),
            pltpu.VMEM((rows, hid), F32),
            pltpu.VMEM((n_dp, depth, rows), BF16),
            pltpu.VMEM((n_dp, depth, rows), BF16),
            pltpu.VMEM((n_dp, depth, rows), BF16),
            pltpu.VMEM((n_dp, depth, hid), BF16),
            pltpu.VMEM((nz, depth, hid), BF16),
            pltpu.VMEM((2, nz, depth, hid), BF16),
            pltpu.VMEM((n_dp, rows, hid), BF16),
            pltpu.SemaphoreType.DMA((4,)),
            pltpu.SemaphoreType.DMA((8, n_tp)),
            pltpu.SemaphoreType.DMA((2, n_dp)),
            pltpu.SemaphoreType.DMA((12, nz)),
        ],
        compiler_params=pltpu.CompilerParams(
            collective_id=0, has_side_effects=True, vmem_limit_bytes=58 * 1024 * 1024
        ),
        name="route_and_grads",
    )(
        row_rank.reshape(1, rows),
        row_rank,
        part,
        padded,
        ln_gain.reshape(1, width),
        ln_bias.reshape(1, width),
        fc1_weight,
        fc1_bias.reshape(1, hid),
        fc2_weight,
    )
    return early[:slots], first, second


def solution(mesh):
    return jax.shard_map(
        shards,
        mesh=mesh,
        in_specs=(
            P("tp", "dp", None),
            P(("dp", "tp"), None),
            P(),
            P(),
            P(None, "tp"),
            P("tp"),
            P(None, "tp"),
            P("dp", None),
        ),
        out_specs=(P(("dp", "tp"), None), P("dp", "tp"), P("dp", "tp")),
        check_vma=False,
    )
```

time: 193 us -> 92.5 us (0.48)
  the two profiles are of different devices: /device:TPU:0 before, /device:TPU:4 now
where the time goes in v1:
time: 92.5 us; the launch traced here: 92 us
  Pallas kernels  78.8 us (85%)
  local copies, waits for them, and re-layouts  12.6 us (14%)
    pallas_call x1, Pallas kernels, shards(): pl.pallas_call(functools.partial(kernel, n_tp, n_dp, share, float(n_dp *...  78.8 us
    unnamed x4, local copies, waits for them, and re-layouts  7.07 us

profile of v1, /device:TPU:4, one launch (start us, length us, event | category | flops | bytes accessed | tf_op | source)
XLA Modules:
  0.0 92.0 jit_solution(7909835978947012958)
XLA Ops:
  0.6 1.3 %reshape.19.gain = f32[1,1280]{1,0:T(1,128)} reshape(f32[1280]{0:T(1024)} %param.10) | data formatting | bytes 10240 | tf_op jit(solution)/shard_map/reshape | solution.py:375
  1.9 1.3 %reshape.20.bias = f32[1,1280]{1,0:T(1,128)} reshape(f32[1280]{0:T(1024)} %param.11) | data formatting | bytes 10240 | tf_op jit(solution)/shard_map/reshape | solution.py:376
  3.2 1.3 %reshape.21.b1 = f32[1,1280]{1,0:T(1,128)} reshape(f32[1280]{0:T(1024)} %param.13) | data formatting | bytes 10240 | tf_op jit(solution)/shard_map/reshape | solution.py:378
  4.5 1.4 %copy.11.rank_col = s32[160,1]{1,0:T(8,128)} copy(s32[160,1]{0,1:T(1,128)} %param.15) | data formatting | bytes 1280 | tf_op args[7]
  5.9 1.6 %pad.4.lin = bf16[64,1280]{1,0:T(8,128)(2,1)} pad(bf16[60,1280]{1,0:T(8,128)(2,1)} %param.9, bf16[]{:T(256)} %constant.2.clone.1), padding=0_4x0_0 | pad | bytes 317442 | tf_op jit(solution)/shard_map/jit(_pad)/pad | solution.py:331
  7.5 78.8 %route_and_grads.1 = (bf16[64,6400]{1,0:T(8,128)(2,1)}, bf16[160,1280]{1,0:T(8,128)(2,1)}, bf16[160,1280]{1,0:T(8,128)(2,1)}) custom-call(s32[1,160]{1,0:T(1,128)} %bitcast.5, s32[160,1]{1,0:T(8,128)} %copy.11.rank_col, bf16[160,7680]{1,0:T(8,128)(2,1)} %bitcast.3, bf16[64,1280]{1,0:T(8,128)(2,1)} %pad.4.lin, f32[1,1280]{1,0:T(1,128)} %reshape.19.gain, ...), custom_call_target="tpu_custom_call" | custom-call | tf_op jit(solution)/shard_map/route_and_grads/pallas_call | solution.py:332
  86.4 2.1 %copy.15 = bf16[60,6400]{1,0:T(8,128)(2,1)} copy(bf16[60,6400]{1,0:T(8,128)(2,1)} %bitcast.4) | data formatting | bytes 1536000
  88.5 1.8 %copy.16 = bf16[160,1280]{1,0:T(8,128)(2,1)} copy(bf16[160,1280]{1,0:T(8,128)(2,1)} %get-tuple-element.13) | data formatting | bytes 819200
  90.3 1.8 %copy.17 = bf16[160,1280]{1,0:T(8,128)(2,1)} copy(bf16[160,1280]{1,0:T(8,128)(2,1)} %get-tuple-element.14) | data formatting | bytes 819200

commit v2 on v1

--- a/solution.py
+++ b/solution.py
@@ -28,9 +28,9 @@
 
 def kernel(
     n_tp, n_dp, share, factor,
-    rank_row, rank_col, part, lin, gain, bias, fc1, b1, fc2,
+    rank_row, part, lin_own, gain, bias, fc1, b1, fc2,
     early_o, g1_o, g2_o,
-    partu, parte, w1, w2, linall, usend, urecv, uall, esend, erecv,
+    partu, parte, w1, w2, lin_wide, lin, linall, usend, urecv, uall, esend, erecv,
     hidden, deriv, nts, ntr, upt, terms, cross, chain, grads,
     lsem, tsem, dsem, zsem,
 ):
@@ -81,6 +81,12 @@
             else:
                 copy.wait_send()
 
+    slots = lin_own.shape[0]
+    lin_wide[0:slots, :] = lin_own[...].astype(F32)
+    if slot_pad > slots:
+        lin_wide[slots:slot_pad, :] = jnp.zeros((slot_pad - slots, width), F32)
+    lin[...] = lin_wide[...].astype(BF16)
+
     own_lin = lambda to: lin
     u_block = lambda to: usend.at[to]
     own_up = lambda to: uall.at[me_tp]
@@ -102,14 +108,15 @@
     tp_send(own_lin, linall, 4)
     linall[me_tp] = lin[...]
 
-    rank_r, rank_c = rank_row[...], rank_col[...]
-    same = rank_c == rank_r
     at0 = lax.broadcasted_iota(jnp.int32, (rows, rows), 0)
     at1 = lax.broadcasted_iota(jnp.int32, (rows, rows), 1)
+    rank_r = rank_row[...].astype(F32)
+    rank_c = jnp.sum(jnp.where(at0 == at1, rank_r, 0.0), axis=1, keepdims=True)
+    same = rank_c == rank_r
     place_r = jnp.sum(jnp.where(same & (at0 < at1), 1.0, 0.0), axis=0, keepdims=True)
     place_c = jnp.sum(jnp.where(same & (at1 < at0), 1.0, 0.0), axis=1, keepdims=True)
-    slot_r = rank_r.astype(F32) * slot_pad + place_r
-    slot_c = rank_c.astype(F32) * slot_pad + place_c
+    slot_r = rank_r * slot_pad + place_r
+    slot_c = rank_c * slot_pad + place_c
     table = onehot(n_tp * slot_pad, rows, slot_r, 0)
     back = onehot(rows, n_tp * slot_pad, slot_c, 1)
 
@@ -135,7 +142,7 @@
     values = fdot(back, linall[...].reshape(n_tp * slot_pad, width))
     centered = values - jnp.mean(values, axis=1, keepdims=True)
     variance = jnp.mean(centered * centered, axis=1, keepdims=True)
-    normed = centered / jnp.sqrt(variance + 1e-05) * gain[...] + bias[...]
+    normed = centered / jnp.sqrt(variance + 1e-05) * gain[...].reshape(1, width) + bias[...].reshape(1, width)
     normed_t = jnp.transpose(normed)
     for d in range(n_dp):
         nts[d] = normed_t[d * depth : (d + 1) * depth].astype(BF16)
@@ -149,7 +156,7 @@
 
     def forward(i, carry):
         columns = pl.ds(pl.multiple_of(i * step_h, step_h), step_h) if step_h != hid else slice(None)
-        preact = fdot(normed, w1[:, columns]) + b1[:, columns]
+        preact = fdot(normed, w1[:, columns]) + b1[columns].reshape(1, step_h)
         cdf = 0.5 * (1.0 + lax.erf(preact * 0.7071067811865476))
         density = jnp.exp(-0.5 * preact * preact) * 0.3989422804014327
         hidden[:, columns] = (preact * cdf).astype(BF16)
@@ -311,6 +318,12 @@
             @pl.when(spot <= step)
             def _():
                 chain_copy(way, real(way, nz - 1 + spot - step)).wait_send()
+
+
+def finish(early, first, second, early_o, first_o, second_o):
+    early_o[...] = early[0 : early_o.shape[0], :]
+    first_o[...] = first[...]
+    second_o[...] = second[...]
 
 
 def shards(partials, layer_input, ln_gain, ln_bias, fc1_weight, fc1_bias, fc2_weight, row_rank):
@@ -328,7 +341,6 @@
     rest = vis - width
     vmem = pl.BlockSpec(memory_space=pltpu.VMEM)
     anywhere = pl.BlockSpec(memory_space=pl.ANY)
-    padded = jnp.pad(layer_input, ((0, slot_pad - slots), (0, 0)))
     early, first, second = pl.pallas_call(
         functools.partial(kernel, n_tp, n_dp, share, float(n_dp * rows) ** (-0.5)),
         out_shape=(
@@ -336,13 +348,15 @@
             jax.ShapeDtypeStruct((depth, hid), BF16),
             jax.ShapeDtypeStruct((depth, hid), BF16),
         ),
-        in_specs=[vmem, vmem, anywhere, vmem, vmem, vmem, anywhere, vmem, anywhere],
+        in_specs=[vmem, anywhere, vmem, vmem, vmem, anywhere, vmem, anywhere],
         out_specs=(vmem, vmem, vmem),
         scratch_shapes=[
             pltpu.VMEM((rows, width), BF16),
             pltpu.VMEM((rows, rest), BF16),
             pltpu.VMEM((width, hid), BF16),
             pltpu.VMEM((width, hid), BF16),
+            pltpu.VMEM((slot_pad, width), F32),
+            pltpu.VMEM((slot_pad, width), BF16),
             pltpu.VMEM((n_tp, slot_pad, width), BF16),
             pltpu.VMEM((n_tp, share_pad, width), BF16),
             pltpu.VMEM((n_tp, share_pad, width), BF16),
@@ -369,16 +383,25 @@
         name="route_and_grads",
     )(
         row_rank.reshape(1, rows),
-        row_rank,
         part,
-        padded,
-        ln_gain.reshape(1, width),
-        ln_bias.reshape(1, width),
+        layer_input,
+        ln_gain,
+        ln_bias,
         fc1_weight,
-        fc1_bias.reshape(1, hid),
+        fc1_bias,
         fc2_weight,
     )
-    return early[:slots], first, second
+    return pl.pallas_call(
+        finish,
+        out_shape=(
+            jax.ShapeDtypeStruct((slots, rest), BF16),
+            jax.ShapeDtypeStruct((depth, hid), BF16),
+            jax.ShapeDtypeStruct((depth, hid), BF16),
+        ),
+        in_specs=[vmem, vmem, vmem],
+        out_specs=(vmem, vmem, vmem),
+        name="finish",
+    )(early, first, second)
 
 
 def solution(mesh):

time: 92.5 us -> 82.2 us (0.89)
  local copies, waits for them, and re-layouts: 12.6 us -> 0 us
  Pallas kernels: 78.8 us -> 81.4 us
    unnamed x4 -> x0, local copies, waits for them, and re-layouts: 7.07 us -> none
    reshape x3 -> x0, local copies, waits for them, and re-layouts: 3.89 us -> none  [the longest x1 1.3 us: shards(): fc1_bias.reshape(1, hid)]
    pallas_call x0 -> x1, Pallas kernels: none -> 2.56 us  [shards(): pl.pallas_call(finish, out_shape=(jax.ShapeDtypeStruct((slots, rest), BF1...]
    pad x1 -> x0, local copies, waits for them, and re-layouts: 1.59 us -> none  [shards(): padded = jnp.pad(layer_input, ((0, slot_pad - slots), (0, 0)))]
where the time goes in v2:
time: 82.2 us; the launch traced here: 82 us
  Pallas kernels  81.4 us (99%)
    pallas_call x1, Pallas kernels, shards(): pl.pallas_call(functools.partial(kernel, n_tp, n_dp, share, float(n_dp *...  78.8 us
    pallas_call x1, Pallas kernels, shards(): pl.pallas_call(finish, out_shape=(jax.ShapeDtypeStruct((slots, rest), BF1...  2.56 us

profile of v2, /device:TPU:4, one launch (start us, length us, event | category | flops | bytes accessed | tf_op | source)
XLA Modules:
  0.0 82.0 jit_solution(14720450567930282744)
XLA Ops:
  0.6 78.8 %route_and_grads.1 = (bf16[64,6400]{1,0:T(8,128)(2,1)}, bf16[160,1280]{1,0:T(8,128)(2,1)}, bf16[160,1280]{1,0:T(8,128)(2,1)}) custom-call(s32[1,160]{1,0:T(1,128)} %bitcast.3, bf16[160,7680]{1,0:T(8,128)(2,1)} %bitcast.2, bf16[60,1280]{1,0:T(8,128)(2,1)} %lin_own.1, f32[1280]{0:T(1024)} %gain.1, f32[1280]{0:T(1024)} %bias.1, bf16[1280,1280]{1,0:T(8,128)(2,1)} %fc1.1, ...), custom_call_target="tpu_custom_call" | custom-call | tf_op jit(solution)/shard_map/route_and_grads/pallas_call | solution.py:344
  79.5 2.6 %finish.1 = (bf16[60,6400]{1,0:T(8,128)(2,1)}, bf16[160,1280]{1,0:T(8,128)(2,1)}, bf16[160,1280]{1,0:T(8,128)(2,1)}) custom-call(bf16[64,6400]{1,0:T(8,128)(2,1)} %get-tuple-element.6.early, bf16[160,1280]{1,0:T(8,128)(2,1)} %get-tuple-element.7.first, bf16[160,1280]{1,0:T(8,128)(2,1)} %get-tuple-element.8.second), custom_call_target="tpu_custom_call" | custom-call | tf_op jit(solution)/shard_map/finish/pallas_call | solution.py:394

commit v3 on v2

--- a/solution.py
+++ b/solution.py
@@ -27,12 +27,12 @@
 
 
 def kernel(
-    n_tp, n_dp, share, factor,
+    n_tp, n_dp, outer, share, factor,
     rank_row, part, lin_own, gain, bias, fc1, b1, fc2,
     early_o, g1_o, g2_o,
-    partu, parte, w1, w2, lin_wide, lin, linall, usend, urecv, uall, esend, erecv,
+    partu, parte, w1, w2, lin_wide, lin, linall, usend, urecv, uall, esend, near, far,
     hidden, deriv, nts, ntr, upt, terms, cross, chain, grads,
-    lsem, tsem, dsem, zsem,
+    lsem, tsem, esem, dsem, zsem,
 ):
     me_tp = lax.axis_index("tp")
     me_dp = lax.axis_index("dp")
@@ -90,7 +90,106 @@
     own_lin = lambda to: lin
     u_block = lambda to: usend.at[to]
     own_up = lambda to: uall.at[me_tp]
-    e_block = lambda to: esend.at[to]
+
+    inner = n_tp // outer
+    place_a, place_b = me_tp // inner, me_tp % inner
+    half = esend.shape[2] // 2
+
+    def axes(way):
+        return ((place_b, inner), (place_a, outer)) if way == 0 else ((place_a, outer), (place_b, inner))
+
+    def rank_of(way, first, second):
+        return second * inner + first if way == 0 else first * inner + second
+
+    def e_half(way, rank):
+        return esend.at[rank, :, pl.ds(way * half, half)]
+
+    def near_copy(way, i, other, sending):
+        (first, extent), (second, count) = axes(way)
+        peer = (first + i) % extent
+        held = first if sending else peer
+        return remote(
+            e_half(way, rank_of(way, peer, other)),
+            near.at[way, held * count + other],
+            esem.at[way, peer * count + other],
+            esem.at[2 + way, held * count + other],
+            {"tp": rank_of(way, peer, second)},
+        )
+
+    def far_copy(way, i, sending):
+        (first, extent), (second, count) = axes(way)
+        peer = (second + i) % count
+        held = second if sending else peer
+        return remote(
+            e_half(way, rank_of(way, first, peer)),
+            far.at[way, held],
+            esem.at[4 + way, peer],
+            esem.at[6 + way, held],
+            {"tp": rank_of(way, first, peer)},
+        )
+
+    def near_all(act):
+        for other in range(n_tp):
+            for way in (0, 1):
+                (_, extent), (_, count) = axes(way)
+                if other < count:
+                    for i in range(1, extent):
+                        act(near_copy(way, i, other, False))
+
+    def near_start():
+        for other in range(n_tp):
+            for way in (0, 1):
+                (_, extent), (_, count) = axes(way)
+                if other < count:
+                    for i in range(1, extent):
+                        near_copy(way, i, other, True).start()
+
+    def near_sum():
+        near_all(lambda copy: copy.wait_recv())
+        for way in (0, 1):
+            (first, extent), (second, count) = axes(way)
+            for i in list(range(1, count)) + [0]:
+                other = (second + i) % count
+                spot = rank_of(way, first, other)
+
+                def add(c, carry):
+                    columns = pl.ds(pl.multiple_of(c * chunk, 128), chunk)
+                    mine = pl.ds(pl.multiple_of(way * half + c * chunk, 128), chunk)
+                    block = esend[spot, :, mine].astype(F32)
+                    for j in range(1, extent):
+                        block = block + near[way, ((first + j) % extent) * count + other, :, columns].astype(F32)
+                    esend[spot, :, mine] = block.astype(BF16)
+                    return carry
+
+                lax.fori_loop(0, half // chunk, add, 0)
+                if i:
+                    far_copy(way, i, True).start()
+
+    def far_sum():
+        for way in (0, 1):
+            (first, extent), (second, count) = axes(way)
+            for i in range(1, count):
+                far_copy(way, i, False).wait_recv()
+
+            def add(c, carry):
+                columns = pl.ds(pl.multiple_of(c * chunk, 128), chunk)
+                mine = pl.ds(pl.multiple_of(way * half + c * chunk, 128), chunk)
+                block = esend[me_tp, :, mine].astype(F32)
+                for j in range(1, count):
+                    block = block + far[way, (second + j) % count, :, columns].astype(F32)
+                early_o[:, mine] = block.astype(BF16)
+                return carry
+
+            lax.fori_loop(0, half // chunk, add, 0)
+
+    def early_sent():
+        near_all(lambda copy: copy.wait_send())
+        for way in (0, 1):
+            _, (_, count) = axes(way)
+            for i in range(1, count):
+                far_copy(way, i, False).wait_send()
+
+    chunk = 640 if half % 640 == 0 else half
 
     r_row = lax.broadcasted_iota(jnp.int32, (1, rows), 1)
     r_col = lax.broadcasted_iota(jnp.int32, (rows, 1), 0)
@@ -136,7 +235,7 @@
         total = total + urecv[(me_tp + i) % n_tp].astype(F32)
     uall[me_tp] = total.astype(BF16)
     tp_send(own_up, uall, 2)
-    tp_send(e_block, erecv, 6)
+    near_start()
 
     tp_wait(own_lin, linall, 4, True)
     values = fdot(back, linall[...].reshape(n_tp * slot_pad, width))
@@ -255,6 +354,8 @@
                 chain[way, owner] = (chain[way, owner].astype(F32) + cross[owner].astype(F32)).astype(BF16)
                 chain_copy(way, owner).start()
 
+        if step == min(1, nz - 2):
+            near_sum()
         for way in (0, 1):
             @pl.when(spots[way] > step)
             def _():
@@ -262,17 +363,7 @@
                 block_copy(way, chip).wait_recv()
                 partner_copy(chip, core).start()
 
-    tp_wait(e_block, erecv, 6, True)
-
-    def collect(i, carry):
-        columns = pl.ds(pl.multiple_of(i * width, 128), width)
-        early = esend[me_tp, :, columns].astype(F32)
-        for j in range(1, n_tp):
-            early = early + erecv[(me_tp + j) % n_tp, :, columns].astype(F32)
-        early_o[:, columns] = early.astype(BF16)
-        return carry
-
-    lax.fori_loop(0, parte.shape[1] // width, collect, 0)
+    far_sum()
 
     for i in range(1, n_dp):
         to = (me_dp + i) % n_dp
@@ -300,7 +391,7 @@
     tp_wait(u_block, urecv, 0, False)
     tp_wait(own_up, uall, 2, False)
     tp_wait(own_lin, linall, 4, False)
-    tp_wait(e_block, erecv, 6, False)
+    early_sent()
     for i in range(1, n_dp):
         to = (me_dp + i) % n_dp
         remote(nts.at[to], ntr.at[to], dsem.at[0, to], dsem.at[1, to], {"dp": to}).wait_send()
@@ -339,10 +430,11 @@
     share_pad = up_to(share, 16)
     depth = width // n_dp
     rest = vis - width
+    outer = max(i for i in range(1, n_tp + 1) if n_tp % i == 0 and i * i <= n_tp)
     vmem = pl.BlockSpec(memory_space=pltpu.VMEM)
     anywhere = pl.BlockSpec(memory_space=pl.ANY)
     early, first, second = pl.pallas_call(
-        functools.partial(kernel, n_tp, n_dp, share, float(n_dp * rows) ** (-0.5)),
+        functools.partial(kernel, n_tp, n_dp, outer, share, float(n_dp * rows) ** (-0.5)),
         out_shape=(
             jax.ShapeDtypeStruct((slot_pad, rest), BF16),
             jax.ShapeDtypeStruct((depth, hid), BF16),
@@ -362,7 +454,8 @@
             pltpu.VMEM((n_tp, share_pad, width), BF16),
             pltpu.VMEM((n_tp, share_pad, width), BF16),
             pltpu.VMEM((n_tp, slot_pad, rest), BF16),
-            pltpu.VMEM((n_tp, slot_pad, rest), BF16),
+            pltpu.VMEM((2, n_tp, slot_pad, rest // 2), BF16),
+            pltpu.VMEM((2, n_tp // outer, slot_pad, rest // 2), BF16),
             pltpu.VMEM((rows, hid), BF16),
             pltpu.VMEM((rows, hid), F32),
             pltpu.VMEM((n_dp, depth, rows), BF16),
@@ -373,6 +466,7 @@
             pltpu.VMEM((2, nz, depth, hid), BF16),
             pltpu.VMEM((n_dp, rows, hid), BF16),
             pltpu.SemaphoreType.DMA((4,)),
+            pltpu.SemaphoreType.DMA((6, n_tp)),
             pltpu.SemaphoreType.DMA((8, n_tp)),
             pltpu.SemaphoreType.DMA((2, n_dp)),
             pltpu.SemaphoreType.DMA((12, nz)),

time: 82.2 us -> 79.4 us (0.966)
  the two profiles are of different devices: /device:TPU:4 before, /device:TPU:0 now
where the time goes in v3:
time: 79.4 us; the launch traced here: 79.2 us
  Pallas kernels  78.6 us (99%)
    pallas_call x1, Pallas kernels, shards(): pl.pallas_call(functools.partial(kernel, n_tp, n_dp, outer, share, float(...  76 us
    pallas_call x1, Pallas kernels, shards(): pl.pallas_call(finish, out_shape=(jax.ShapeDtypeStruct((slots, rest), BF1...  2.56 us

profile of v3, /device:TPU:0, one launch (start us, length us, event | category | flops | bytes accessed | tf_op | source)
XLA Modules:
  0.0 79.2 jit_solution(13436350869077583595)
XLA Ops:
  0.6 76.0 %route_and_grads.1 = (bf16[64,6400]{1,0:T(8,128)(2,1)}, bf16[160,1280]{1,0:T(8,128)(2,1)}, bf16[160,1280]{1,0:T(8,128)(2,1)}) custom-call(s32[1,160]{1,0:T(1,128)} %bitcast.3, bf16[160,7680]{1,0:T(8,128)(2,1)} %bitcast.2, bf16[60,1280]{1,0:T(8,128)(2,1)} %lin_own.1, f32[1280]{0:T(1024)} %gain.1, f32[1280]{0:T(1024)} %bias.1, bf16[1280,1280]{1,0:T(8,128)(2,1)} %fc1.1, ...), custom_call_target="tpu_custom_call" | custom-call | tf_op jit(solution)/shard_map/route_and_grads/pallas_call | solution.py:436
  76.6 2.6 %finish.1 = (bf16[60,6400]{1,0:T(8,128)(2,1)}, bf16[160,1280]{1,0:T(8,128)(2,1)}, bf16[160,1280]{1,0:T(8,128)(2,1)}) custom-call(bf16[64,6400]{1,0:T(8,128)(2,1)} %get-tuple-element.6.early, bf16[160,1280]{1,0:T(8,128)(2,1)} %get-tuple-element.7.first, bf16[160,1280]{1,0:T(8,128)(2,1)} %get-tuple-element.8.second), custom_call_target="tpu_custom_call" | custom-call | tf_op jit(solution)/shard_map/finish/pallas_call | solution.py:488

commit v4 on v3

--- a/solution.py
+++ b/solution.py
@@ -27,7 +27,7 @@
 
 
 def kernel(
-    n_tp, n_dp, outer, share, factor,
+    n_tp, n_dp, outer, pieces, share, factor,
     rank_row, part, lin_own, gain, bias, fc1, b1, fc2,
     early_o, g1_o, g2_o,
     partu, parte, w1, w2, lin_wide, lin, linall, usend, urecv, uall, esend, near, far,
@@ -283,13 +283,18 @@
     def real(way, at):
         return at if way == 0 else nz - 1 - at
 
-    def block_copy(way, chip):
-        block = grads.at[chip * CORES + core]
-        return remote(block, block, zsem.at[way, chip], zsem.at[2 + way, chip], ahead[way])
-
-    def chain_copy(way, owner):
-        block = chain.at[way, owner]
-        return remote(block, block, zsem.at[4 + way, owner], zsem.at[6 + way, owner], ahead[way])
+    def part_of(extent, piece):
+        return pl.ds(piece * (extent // pieces), extent // pieces)
+
+    def block_copy(way, chip, piece):
+        block = grads.at[chip * CORES + core, part_of(rows, piece)]
+        at = chip * pieces + piece
+        return remote(block, block, zsem.at[way, at], zsem.at[2 + way, at], ahead[way])
+
+    def chain_copy(way, owner, piece):
+        block = chain.at[way, owner, part_of(depth, piece)]
+        at = owner * pieces + piece
+        return remote(block, block, zsem.at[4 + way, at], zsem.at[6 + way, at], ahead[way])
 
     def partner_copy(chip, side):
         block = grads.at[chip * CORES + side]
@@ -300,14 +305,11 @@
             terms.at[chip * CORES + 1 - core], cross.at[chip], zsem.at[10, chip], zsem.at[11, chip], partner
         )
 
-    def send_block(step):
+    for piece in range(pieces):
         for way in (0, 1):
-            @pl.when((spots[way] >= step) & (spots[way] < nz - 1))
+            @pl.when(spots[way] < nz - 1)
             def _():
-                block_copy(way, real(way, spots[way] - step)).start()
-
-    send_block(0)
-    partner_copy(z, core).start()
+                block_copy(way, z, piece).start()
 
     up_t = jnp.transpose(up_f)
     for d in range(n_dp):
@@ -326,6 +328,7 @@
         return carry
 
     lax.fori_loop(0, nz, other_terms, 0)
+    partner_copy(z, core).start()
     lax.fori_loop(0, nz, own_terms, 0)
 
     def merge(chip, carry):
@@ -337,31 +340,44 @@
     lax.fori_loop(0, nz, merge, 0)
 
     for step in range(nz - 1):
-        if step:
-            send_block(step)
-        for way in (0, 1):
-            spot = spots[way]
-            owner = real(way, nz - 1 + spot - step)
-
-            @pl.when((spot <= step) & (spot == 0))
-            def _():
-                chain[way, owner] = cross[owner]
-                chain_copy(way, owner).start()
-
-            @pl.when((spot <= step) & (spot > 0))
-            def _():
-                chain_copy(way, owner).wait_recv()
-                chain[way, owner] = (chain[way, owner].astype(F32) + cross[owner].astype(F32)).astype(BF16)
-                chain_copy(way, owner).start()
-
-        if step == min(1, nz - 2):
+        for piece in range(pieces):
+            part_rows = part_of(depth, piece)
+            for way in (0, 1):
+                spot = spots[way]
+                owner = real(way, nz - 1 + spot - step)
+
+                @pl.when((spot <= step) & (spot == 0))
+                def _():
+                    chain[way, owner, part_rows] = cross[owner, part_rows]
+                    chain_copy(way, owner, piece).start()
+
+                @pl.when((spot <= step) & (spot > 0))
+                def _():
+                    chain_copy(way, owner, piece).wait_recv()
+                    chain[way, owner, part_rows] = (
+                        chain[way, owner, part_rows].astype(F32) + cross[owner, part_rows].astype(F32)
+                    ).astype(BF16)
+                    chain_copy(way, owner, piece).start()
+
+            for way in (0, 1):
+                chip = real(way, spots[way] - 1 - step)
+
+                @pl.when(spots[way] > step)
+                def _():
+                    block_copy(way, chip, piece).wait_recv()
+
+                @pl.when((spots[way] > step) & (spots[way] < nz - 1))
+                def _():
+                    block_copy(way, chip, piece).start()
+
+            if piece == pieces - 1:
+                for way in (0, 1):
+                    @pl.when(spots[way] > step)
+                    def _():
+                        partner_copy(real(way, spots[way] - 1 - step), core).start()
+
+        if step == 0:
             near_sum()
-        for way in (0, 1):
-            @pl.when(spots[way] > step)
-            def _():
-                chip = real(way, spots[way] - 1 - step)
-                block_copy(way, chip).wait_recv()
-                partner_copy(chip, core).start()
 
     far_sum()
 
@@ -379,7 +395,8 @@
     for way in (0, 1):
         @pl.when(spots[way] > 0)
         def _():
-            chain_copy(way, z).wait_recv()
+            for piece in range(pieces):
+                chain_copy(way, z, piece).wait_recv()
 
         @pl.when(spots[way] == 0)
         def _():
@@ -399,16 +416,17 @@
         partner_copy(chip, core).wait_send()
         cross_copy(chip).wait_send()
     for step in range(nz - 1):
-        for way in (0, 1):
-            spot = spots[way]
-
-            @pl.when((spot >= step) & (spot < nz - 1))
-            def _():
-                block_copy(way, real(way, spot - step)).wait_send()
-
-            @pl.when(spot <= step)
-            def _():
-                chain_copy(way, real(way, nz - 1 + spot - step)).wait_send()
+        for piece in range(pieces):
+            for way in (0, 1):
+                spot = spots[way]
+
+                @pl.when((spot >= step) & (spot < nz - 1))
+                def _():
+                    block_copy(way, real(way, spot - step), piece).wait_send()
+
+                @pl.when(spot <= step)
+                def _():
+                    chain_copy(way, real(way, nz - 1 + spot - step), piece).wait_send()
 
 
 def finish(early, first, second, early_o, first_o, second_o):
@@ -430,11 +448,12 @@
     share_pad = up_to(share, 16)
     depth = width // n_dp
     rest = vis - width
+    pieces = 2 if depth % 32 == 0 and rows % 32 == 0 else 1
     outer = max(i for i in range(1, n_tp + 1) if n_tp % i == 0 and i * i <= n_tp)
     vmem = pl.BlockSpec(memory_space=pltpu.VMEM)
     anywhere = pl.BlockSpec(memory_space=pl.ANY)
     early, first, second = pl.pallas_call(
-        functools.partial(kernel, n_tp, n_dp, outer, share, float(n_dp * rows) ** (-0.5)),
+        functools.partial(kernel, n_tp, n_dp, outer, pieces, share, float(n_dp * rows) ** (-0.5)),
         out_shape=(
             jax.ShapeDtypeStruct((slot_pad, rest), BF16),
             jax.ShapeDtypeStruct((depth, hid), BF16),
@@ -469,7 +488,7 @@
             pltpu.SemaphoreType.DMA((6, n_tp)),
             pltpu.SemaphoreType.DMA((8, n_tp)),
             pltpu.SemaphoreType.DMA((2, n_dp)),
-            pltpu.SemaphoreType.DMA((12, nz)),
+            pltpu.SemaphoreType.DMA((12, nz * pieces)),
         ],
         compiler_params=pltpu.CompilerParams(
             collective_id=0, has_side_effects=True, vmem_limit_bytes=58 * 1024 * 1024

time: 79.4 us -> 76 us (0.957)
  Pallas kernels: 78.6 us -> 74.6 us
    pallas_call x1, Pallas kernels: 76 us -> 72.1 us  [shards(): pl.pallas_call(functools.partial(kernel, n_tp, n_dp, outer, pieces, share...]
where the time goes in v4:
time: 76 us; the launch traced here: 75.3 us
  Pallas kernels  74.6 us (98%)
    pallas_call x1, Pallas kernels, shards(): pl.pallas_call(functools.partial(kernel, n_tp, n_dp, outer, pieces, share...  72.1 us
    pallas_call x1, Pallas kernels, shards(): pl.pallas_call(finish, out_shape=(jax.ShapeDtypeStruct((slots, rest), BF1...  2.56 us

profile of v4, /device:TPU:0, one launch (start us, length us, event | category | flops | bytes accessed | tf_op | source)
XLA Modules:
  0.0 75.3 jit_solution(14593773175951543993)
XLA Ops:
  0.6 72.1 %route_and_grads.1 = (bf16[64,6400]{1,0:T(8,128)(2,1)}, bf16[160,1280]{1,0:T(8,128)(2,1)}, bf16[160,1280]{1,0:T(8,128)(2,1)}) custom-call(s32[1,160]{1,0:T(1,128)} %bitcast.3, bf16[160,7680]{1,0:T(8,128)(2,1)} %bitcast.2, bf16[60,1280]{1,0:T(8,128)(2,1)} %lin_own.1, f32[1280]{0:T(1024)} %gain.1, f32[1280]{0:T(1024)} %bias.1, bf16[1280,1280]{1,0:T(8,128)(2,1)} %fc1.1, ...), custom_call_target="tpu_custom_call" | custom-call | tf_op jit(solution)/shard_map/route_and_grads/pallas_call | solution.py:455
  72.7 2.6 %finish.1 = (bf16[60,6400]{1,0:T(8,128)(2,1)}, bf16[160,1280]{1,0:T(8,128)(2,1)}, bf16[160,1280]{1,0:T(8,128)(2,1)}) custom-call(bf16[64,6400]{1,0:T(8,128)(2,1)} %get-tuple-element.6.early, bf16[160,1280]{1,0:T(8,128)(2,1)} %get-tuple-element.7.first, bf16[160,1280]{1,0:T(8,128)(2,1)} %get-tuple-element.8.second), custom_call_target="tpu_custom_call" | custom-call | tf_op jit(solution)/shard_map/finish/pallas_call | solution.py:507
